TPU v7x, 512 devices: a whole 4x8x8 slice. The times are simulated.
512 devices in a mesh: dp: 32 (over z, x), tensor: 16 (over y, core).
Axes of the slice: x: 4, y: 8, z: 8, core: 2. Of those that a mesh axis runs over, the one named last changes fastest.
Arguments:
- hidden: bfloat16 [8192, 2, 8192], P('dp', None, 'tensor'), may hold values from -6 to 6
- key_value_weight: bfloat16 [8192, 2048], P('tensor'), may hold values from -0.0625 to 0.0625
- adapter_down_weight: bfloat16 [512, 8192, 64], P('dp', 'tensor'), may hold values from -0.0625 to 0.0625
- adapter_up_weight: bfloat16 [512, 64, 2048], P('dp', None, 'tensor'), may hold values from -0.75 to 0.75
- attempt_adapter_slot: int32 [8192, 1], P('dp'), may hold values from 0 to 31; in each aligned block of 256 rows (0 to 255, 256 to 511, ...) at most 32 rows name the same one
- group_slot_task: int32 [32, 32], replicated, may hold values from 0 to 511, as said below
- task_row_position: int32 [512], replicated, may hold values from 0 to 511, as said below
- scores: int32 [8192], P('dp'), may hold values 0 or 1
- cotangent: bfloat16 [8192, 2, 2048], P('dp', None, 'tensor'), may hold values from -6 to 6
Outputs:
- kv_new: bfloat16 [8192, 2, 2048], P('dp', None, 'tensor')
- grad_down: bfloat16 [512, 8192, 64], P('dp', 'tensor')
- grad_up: bfloat16 [512, 64, 2048], P('dp', None, 'tensor')
Inputs may be any that keep to these rules, and one draw needn't show every extreme that they name: `attempt_adapter_slot`: among the 256 attempts of one group (aligned blocks of 256 rows), at most 32 name the same slot, and exactly 32 do in some block. `task_row_position`: every row is named once; rows o * 16 to (o + 1) * 16 - 1 belong to group o. group_slot_task[g, o] is a task t with task_row_position[t] between o * 16 and (o + 1) * 16 - 1.
All inputs are finite; a program needn't handle non-finite values. No bound on the sum of `scores` on one device may be relied on, other than what follows from the above.
Results may differ from a plain program's by a relative error of at most 0.0057.
Values may be sent and summed in bfloat16 or wider, within the bound.
A program may use at most 64 MiB of HBM per device.

v0:
```python
import jax
import jax.numpy as jnp
from jax import lax
from jax.sharding import PartitionSpec as P

adapter_output_scale = 0.25


def body(
    hidden,
    key_value_weight,
    adapter_down_weight,
    adapter_up_weight,
    attempt_adapter_slot,
    group_slot_task,
    task_row_position,
    scores,
    cotangent,
):
    groups = lax.axis_size("dp")
    me = lax.axis_index("dp")
    att, steps, width = hidden.shape
    task_dev, _, rank = adapter_down_weight.shape
    kv = cotangent.shape[2]
    most = att // 8
    bf16, f32 = (jnp.bfloat16, jnp.float32)
    slot = attempt_adapter_slot[:, 0]
    ids = jnp.arange(groups, dtype=jnp.int32)
    hot = slot[:, None] == ids[None, :]
    order = jnp.arange(att, dtype=jnp.int32)
    earlier = (order[:, None] > order[None, :]) & (slot[:, None] == slot[None, :])
    place = slot * most + jnp.sum(earlier.astype(jnp.int32), axis=1)
    pick = jnp.arange(groups * most, dtype=jnp.int32)[:, None] == place[None, :]
    pick_bf = pick.astype(bf16)
    hid_out = jnp.einsum("pa,asd->psd", pick_bf, hidden, preferred_element_type=f32).astype(bf16)
    cot_out = jnp.einsum("pa,ask->psk", pick_bf, cotangent, preferred_element_type=f32).astype(bf16)
    mark_out = jnp.sum(
        jnp.where(pick[:, None, :], jnp.stack([scores, jnp.ones_like(scores)])[None], 0), axis=2
    ).astype(f32)
    mark_out = mark_out.reshape(groups, most, 2)

    def swap(x):
        return lax.all_to_all(x, "dp", split_axis=0, concat_axis=0, tiled=True)

    marks = swap(mark_out)
    hid = swap(hid_out.reshape(groups, most, steps, width))
    cot = swap(cot_out.reshape(groups, most, steps, kv))
    base_terms = jnp.einsum("asd,dk->ask", hidden, key_value_weight, preferred_element_type=f32)
    base = lax.psum_scatter(base_terms, "tensor", scatter_dimension=2, tiled=True)
    task_of = lax.dynamic_index_in_dim(group_slot_task, me, 1, keepdims=False)
    task_ids = jnp.arange(task_row_position.shape[0], dtype=jnp.int32)
    stored = jnp.sum(
        jnp.where(task_of[:, None] == task_ids[None, :], task_row_position[None, :], 0), axis=1
    )
    local = stored % task_dev
    local_hot = local[:, None] == jnp.arange(task_dev, dtype=jnp.int32)[None, :]
    same = (local[:, None] == local[None, :]).astype(f32)
    sums = jnp.sum(same[:, :, None] * jnp.sum(marks, axis=1)[None], axis=1)
    mean = sums[:, 0] / jnp.maximum(sums[:, 1], 1.0)
    advantage = marks[:, :, 0] - mean[:, None] * marks[:, :, 1]
    weighted = (advantage[:, :, None, None] * cot.astype(f32)).astype(bf16)
    down = jnp.take(adapter_down_weight, local, axis=0)
    up = jnp.take(adapter_up_weight, local, axis=0)
    inner_down = jnp.einsum("gjsd,gdr->gjsr", hid, down, preferred_element_type=f32)
    inner_back = jnp.einsum("gjsk,grk->gjsr", weighted, up, preferred_element_type=f32)
    inner = lax.psum(jnp.concatenate([inner_down, inner_back], axis=3), "tensor").astype(bf16)
    inner_down, inner_back = (inner[..., :rank], inner[..., rank:])
    delta = (
        adapter_output_scale
        * jnp.einsum("gjsr,grk->gjsk", inner_down, up, preferred_element_type=f32)
    ).astype(bf16)
    delta = swap(delta)
    spread = jnp.where(local_hot[:, None, None, :, None], inner_back[:, :, :, None, :], 0)
    grad_down = jnp.einsum("gjsd,gjstr->tdr", hid, spread, preferred_element_type=f32)
    spread = jnp.where(local_hot[:, None, None, :, None], inner_down[:, :, :, None, :], 0)
    grad_up = jnp.einsum("gjstr,gjsk->trk", spread, weighted, preferred_element_type=f32)
    grad_down = (adapter_output_scale * grad_down).astype(bf16)
    grad_up = (adapter_output_scale * grad_up).astype(bf16)
    mine = jnp.einsum(
        "pa,psk->ask", pick_bf, delta.reshape(groups * most, steps, kv), preferred_element_type=f32
    )
    return ((base + mine).astype(bf16), grad_down, grad_up)


def solution(mesh):
    in_specs = (
        P("dp", None, "tensor"),
        P("tensor", None),
        P("dp", "tensor", None),
        P("dp", None, "tensor"),
        P("dp", None),
        P(),
        P(),
        P("dp"),
        P("dp", None, "tensor"),
    )
    out_specs = (P("dp", None, "tensor"), P("dp", "tensor", None), P("dp", None, "tensor"))
    return jax.shard_map(body, mesh=mesh, in_specs=in_specs, out_specs=out_specs, check_vma=False)
```

profile of v0, /device:TPU:26, one launch (start us, length us, event | category | flops | bytes accessed | tf_op | source)
XLA Modules:
  0.0 209.4 jit_solution(15004701261736432002)
XLA Ops:
  7.2 1.5 copy-done
  8.8 4.2 %fusion.14 = f32[256,2,2048]{2,0,1:T(8,128)} fusion(bf16[512,2048]{1,0:T(8,128)(2,1)S(1)} %copy-done, bf16[256,2,512]{2,1,0:T(2,128)(2,1)} %param.9), kind=kOutput, calls=%fused_computation.17 | convolution fusion | flops 1073741824 | bytes 6815744 | tf_op jit(solution)/shard_map/asd,dk->ask/dot_general | solution.py:48
  15.7 13.5 %all-to-all-start.1 = ((f32[32,32,2]{1,2,0:T(2,128)}), f32[32,32,2]{1,2,0:T(2,128)S(1)}, u32[]{:S(2)}, u32[]{:S(2)}) async-start(f32[32,32,2]{1,2,0:T(2,128)} %copy.63), calls=%async_computation.2 | async-start | bytes 65536 | tf_op jit(solution)/shard_map/all_to_all | solution.py:43
  29.8 0.9 copy.68
  30.6 7.2 %all-to-all-done.1 = f32[32,32,2]{1,2,0:T(2,128)S(1)} async-done(((f32[32,32,2]{1,2,0:T(2,128)}), f32[32,32,2]{1,2,0:T(2,128)S(1)}, u32[]{:S(2)}, u32[]{:S(2)}) %all-to-all-start.1) | async-done | bytes 8224 | tf_op jit(solution)/shard_map/all_to_all | solution.py:43
  37.8 5.6 %all-to-all-start.2 = ((bf16[32,32,2,128]{3,1,2,0:T(8,128)(2,1)}), bf16[32,32,2,128]{3,1,2,0:T(8,128)(2,1)}, u32[]{:S(2)}, u32[]{:S(2)}) async-start(bf16[32,32,2,128]{3,1,2,0:T(8,128)(2,1)} %copy.68), calls=%async_computation.3 | async-start | bytes 1048576 | tf_op jit(solution)/shard_map/all_to_all | solution.py:43
  43.5 0.8 convolution_convert_fusion
  44.3 1.6 copy.61
  45.9 13.4 %all-to-all-done.2 = bf16[32,32,2,128]{3,1,2,0:T(8,128)(2,1)} async-done(((bf16[32,32,2,128]{3,1,2,0:T(8,128)(2,1)}), bf16[32,32,2,128]{3,1,2,0:T(8,128)(2,1)}, u32[]{:S(2)}, u32[]{:S(2)}) %all-to-all-start.2) | async-done | bytes 524320 | tf_op jit(solution)/shard_map/all_to_all | solution.py:43
  59.3 6.0 %all-to-all-start = ((bf16[32,32,2,512]{3,1,2,0:T(8,128)(2,1)}), bf16[32,32,2,512]{3,1,2,0:T(8,128)(2,1)}, u32[]{:S(2)}, u32[]{:S(2)}) async-start(bf16[32,32,2,512]{3,1,2,0:T(8,128)(2,1)} %copy.61), calls=%async_computation.1 | async-start | bytes 4194304 | tf_op jit(solution)/shard_map/all_to_all | solution.py:43
  65.8 1.4 gather_fusion.1
  67.2 2.1 gather_fusion
  69.8 1.7 fusion.44
  71.5 41.9 %all-to-all-done = bf16[32,32,2,512]{3,1,2,0:T(8,128)(2,1)} async-done(((bf16[32,32,2,512]{3,1,2,0:T(8,128)(2,1)}), bf16[32,32,2,512]{3,1,2,0:T(8,128)(2,1)}, u32[]{:S(2)}, u32[]{:S(2)}) %all-to-all-start) | async-done | bytes 2097184 | tf_op jit(solution)/shard_map/all_to_all | solution.py:43
  113.4 3.0 %fusion.12 = f32[32,32,2,64]{3,1,2,0:T(8,128)S(1)} fusion(bf16[32,32,2,512]{3,1,2,0:T(8,128)(2,1)} %all-to-all-done, bf16[32,512,64]{1,2,0:T(8,128)(2,1)} %gather_fusion, pred[32]{0:T(512)(128)(4,1)S(1)} %get-tuple-element.18), kind=kOutput, calls=%fused_computation.15 | convolution fusion | flops 135266304 | bytes 4718624 | tf_op jit(solution)/shard_map/gjsd,gdr->gjsr/dot_general | solution.py:64
  116.4 1.3 pad_maximum_fusion
  117.7 56.3 %all-reduce.2 = bf16[32,32,2,128]{3,1,2,0:T(8,128)(2,1)S(1)} all-reduce(f32[32,32,2,128]{3,1,2,0:T(8,128)} %pad_maximum_fusion), channel_id=1, replica_groups=mesh['dp'=32,'tensor'=16] {'tensor'}, use_global_device_ids=true, to_apply=%region_6.7 | all-reduce | flops 262144 | bytes 1572864 | tf_op jit(solution)/shard_map/psum | solution.py:66
  174.1 2.2 %fusion.27 = bf16[32,32,2,128]{3,1,2,0:T(8,128)(2,1)} fusion(bf16[32,64,128]{2,1,0:T(8,128)(2,1)} %gather_fusion.1, pred[32]{0:T(512)(128)(4,1)S(1)} %get-tuple-element.18, bf16[32,32,2,128]{3,1,2,0:T(8,128)(2,1)S(1)} %all-reduce.2), kind=kOutput, calls=%fused_computation.26 | convolution fusion | flops 34340864 | bytes 1572896 | tf_op jit(solution)/shard_map/gjsr,grk->gjsk/dot_general | solution.py:70
  176.3 6.3 %all-to-all-start.3 = ((bf16[32,32,2,128]{3,1,2,0:T(8,128)(2,1)}), bf16[32,32,2,128]{3,1,2,0:T(8,128)(2,1)S(1)}, u32[]{:S(2)}, u32[]{:S(2)}) async-start(bf16[32,32,2,128]{3,1,2,0:T(8,128)(2,1)} %fusion.27), calls=%async_computation.4 | async-start | bytes 1048576 | tf_op jit(solution)/shard_map/all_to_all | solution.py:43
  182.8 7.1 %fusion.22 = bf16[16,512,64]{1,2,0:T(8,128)(2,1)} fusion(bf16[32,32,2,512]{3,1,2,0:T(8,128)(2,1)} %all-to-all-done, pred[32,16]{1,0:T(8,128)(4,1)S(1)} %iota_compare_fusion.6, bf16[32,32,2,64]{3,1,2,0:T(8,128)(2,1)S(1)} %get-tuple-element.21), kind=kOutput, calls=%fused_computation.24 | convolution fusion | flops 2150629376 | bytes 3408384 | tf_op jit(solution)/shard_map/gjsd,gjstr->tdr/dot_general | solution.py:74
  189.9 4.9 %fusion.34 = bf16[16,64,128]{2,1,0:T(8,128)(2,1)} fusion(pred[32,16]{1,0:T(8,128)(4,1)S(1)} %iota_compare_fusion.6, bf16[32,32,2,64]{3,1,2,0:T(8,128)(2,1)S(1)} %get-tuple-element.20, bf16[32,32,2,128]{3,1,2,0:T(8,128)(2,1)} %all-to-all-done.2, f32[32,32]{1,0:T(8,128)S(1)} %multiply_subtract_fusion), kind=kOutput, calls=%fused_computation.29 | convolution fusion | flops 540016640 | bytes 1053184 | tf_op jit(solution)/shard_map/gjstr,gjsk->trk/dot_general | solution.py:76
  194.8 5.7 %all-to-all-done.3 = bf16[32,32,2,128]{3,1,2,0:T(8,128)(2,1)S(1)} async-done(((bf16[32,32,2,128]{3,1,2,0:T(8,128)(2,1)}), bf16[32,32,2,128]{3,1,2,0:T(8,128)(2,1)S(1)}, u32[]{:S(2)}, u32[]{:S(2)}) %all-to-all-start.3) | async-done | bytes 524320 | tf_op jit(solution)/shard_map/all_to_all | solution.py:43
  200.5 1.3 fusion.37
  201.8 0.8 copy.70
  (45 shorter events, 4.5 us)
Async XLA Ops:
  7.2 1.6 copy-start
  7.2 193.3 %reduce-scatter.2.cloned.1.call-start = ((), (), s32[]{:S(2)}) async-start(), calls=%async_computation.5 | async-start | bytes 4456448 | tf_op jit(solution)/shard_map/reduce_scatter | solution.py:49
  13.0 0.7 copy-start.5
  13.0 1.5 copy-start.7
  13.0 16.2 %copy-start.8 = (bf16[256,2,128]{2,1,0:T(2,128)(2,1)S(1)}, bf16[256,2,128]{2,1,0:T(2,128)(2,1)}, u32[]{:S(2)}) copy-start(bf16[256,2,128]{2,1,0:T(2,128)(2,1)} %param.17) | copy-start | bytes 393220
  13.0 30.5 %copy-start.2 = (bf16[256,2,512]{2,1,0:T(2,128)(2,1)S(1)}, bf16[256,2,512]{2,1,0:T(2,128)(2,1)}, u32[]{:S(2)}) copy-start(bf16[256,2,512]{2,1,0:T(2,128)(2,1)} %param.9) | copy-start | bytes 1572868
  15.7 22.1 %all-to-all-start.1 = ((f32[32,32,2]{1,2,0:T(2,128)}), f32[32,32,2]{1,2,0:T(2,128)S(1)}, u32[]{:S(2)}, u32[]{:S(2)}) async-start(f32[32,32,2]{1,2,0:T(2,128)} %copy.63), calls=%async_computation.2 | async-start | bytes 65536 | tf_op jit(solution)/shard_map/all_to_all | solution.py:43
  37.8 21.5 %all-to-all-start.2 = ((bf16[32,32,2,128]{3,1,2,0:T(8,128)(2,1)}), bf16[32,32,2,128]{3,1,2,0:T(8,128)(2,1)}, u32[]{:S(2)}, u32[]{:S(2)}) async-start(bf16[32,32,2,128]{3,1,2,0:T(8,128)(2,1)} %copy.68), calls=%async_computation.3 | async-start | bytes 1048576 | tf_op jit(solution)/shard_map/all_to_all | solution.py:43
  45.9 19.4 %copy-start.4 = (s32[32,32]{1,0:T(8,128)S(1)}, s32[32,32]{1,0:T(8,128)}, u32[]{:S(2)}) copy-start(s32[32,32]{1,0:T(8,128)} %param.14) | copy-start | bytes 12292
  45.9 19.6 %copy-start.6 = (s32[512]{0:T(512)S(1)}, s32[512]{0:T(512)}, u32[]{:S(2)}) copy-start(s32[512]{0:T(512)} %param.15) | copy-start | bytes 6148
  45.9 19.8 %copy-start.3 = (bf16[16,64,128]{2,1,0:T(8,128)(2,1)S(1)}, bf16[16,64,128]{2,1,0:T(8,128)(2,1)}, u32[]{:S(2)}) copy-start(bf16[16,64,128]{2,1,0:T(8,128)(2,1)} %param.12) | copy-start | bytes 786436
  45.9 21.3 %copy-start.1 = (bf16[16,512,64]{1,2,0:T(8,128)(2,1)S(1)}, bf16[16,512,64]{1,2,0:T(8,128)(2,1)}, u32[]{:S(2)}) copy-start(bf16[16,512,64]{1,2,0:T(8,128)(2,1)} %param.11) | copy-start | bytes 3145732
  59.3 54.1 %all-to-all-start = ((bf16[32,32,2,512]{3,1,2,0:T(8,128)(2,1)}), bf16[32,32,2,512]{3,1,2,0:T(8,128)(2,1)}, u32[]{:S(2)}, u32[]{:S(2)}) async-start(bf16[32,32,2,512]{3,1,2,0:T(8,128)(2,1)} %copy.61), calls=%async_computation.1 | async-start | bytes 4194304 | tf_op jit(solution)/shard_map/all_to_all | solution.py:43
  176.3 24.1 %all-to-all-start.3 = ((bf16[32,32,2,128]{3,1,2,0:T(8,128)(2,1)}), bf16[32,32,2,128]{3,1,2,0:T(8,128)(2,1)S(1)}, u32[]{:S(2)}, u32[]{:S(2)}) async-start(bf16[32,32,2,128]{3,1,2,0:T(8,128)(2,1)} %fusion.27), calls=%async_computation.4 | async-start | bytes 1048576 | tf_op jit(solution)/shard_map/all_to_all | solution.py:43
Sparse Core Ops, SparseCore 0:
  13.1 67.2 reduce-scatter.1
where the time goes:
time: 210 us; the launch traced here: 209 us
  waiting for transfers between devices  68.2 us (32%)
  blocking collectives  56.3 us (27%)
  starting transfers between devices  31.4 us (15%)
  matrix products  25.7 us (12%)
  between operations  14.3 us (7%)
  local copies, waits for them, and re-layouts  10.7 us (5%)
  other arithmetic  2.78 us (1%)
    all_to_all x4, waiting for transfers between devices, swap(): return lax.all_to_all(x, 'dp', split_axis=0, concat_axis=0, tiled=True)  68.1 us
    psum x1, blocking collectives, body(): lax.psum(jnp.concatenate([inner_down, inner_back], axis=3), 'tensor')  56.3 us
    all_to_all x4, starting transfers between devices, swap(): return lax.all_to_all(x, 'dp', split_axis=0, concat_axis=0, tiled=True)  31.4 us
    dot_general x1, matrix products, body(): jnp.einsum('gjsd,gjstr->tdr', hid, spread, preferred_element_type=f32)  7.06 us
    dot_general x1, matrix products, body(): jnp.einsum('gjstr,gjsk->trk', spread, weighted, preferred_element_type=f32)  4.87 us
    dot_general x1, matrix products, body(): jnp.einsum('asd,dk->ask', hidden, key_value_weight, preferred_element_typ...  4.22 us
  transfers between devices with their start and end apart: 5, of which 4 were waited for; matrix products, arithmetic and copies ran while one was open for 15% of the time, Pallas kernels for 0%

commit v1 on v0

--- a/solution.py
+++ b/solution.py
@@ -63,7 +63,9 @@
     up = jnp.take(adapter_up_weight, local, axis=0)
     inner_down = jnp.einsum("gjsd,gdr->gjsr", hid, down, preferred_element_type=f32)
     inner_back = jnp.einsum("gjsk,grk->gjsr", weighted, up, preferred_element_type=f32)
-    inner = lax.psum(jnp.concatenate([inner_down, inner_back], axis=3), "tensor").astype(bf16)
+    inner = jnp.sum(
+        lax.all_gather(jnp.concatenate([inner_down, inner_back], axis=3), "tensor"), axis=0
+    ).astype(bf16)
     inner_down, inner_back = (inner[..., :rank], inner[..., rank:])
     delta = (
         adapter_output_scale

time: 210 us -> 286 us (1.36)
  the two profiles are of different devices: /device:TPU:26 before, /device:TPU:25 now
where the time goes in v1:
time: 286 us; the launch traced here: 285 us
  waiting for transfers between devices  190 us (66%)
  starting transfers between devices  34.1 us (12%)
  matrix products  25.6 us (9%)
  between operations  14.3 us (5%)
  other arithmetic  12.2 us (4%)
  local copies, waits for them, and re-layouts  9.13 us (3%)
    all_gather x1, waiting for transfers between devices, body(): lax.all_gather(jnp.concatenate([inner_down, inner_back], axis=3), 'tensor')  95.3 us
    all_to_all x4, waiting for transfers between devices, swap(): return lax.all_to_all(x, 'dp', split_axis=0, concat_axis=0, tiled=True)  62.5 us
    all_to_all x4, starting transfers between devices, swap(): return lax.all_to_all(x, 'dp', split_axis=0, concat_axis=0, tiled=True)  34 us
    reduce_scatter x1, waiting for transfers between devices, body(): lax.psum_scatter(base_terms, 'tensor', scatter_dimension=2, tiled=True)  31.9 us
    reduce_sum x1, other arithmetic, body(): jnp.sum(lax.all_gather(jnp.concatenate([inner_down, inner_back], axis=3),...  7.94 us
    dot_general x1, matrix products, body(): jnp.einsum('gjsd,gjstr->tdr', hid, spread, preferred_element_type=f32)  7.06 us
  transfers between devices with their start and end apart: 6, of which 6 were waited for; matrix products, arithmetic and copies ran while one was open for 13% of the time, Pallas kernels for 0%

profile of v1, /device:TPU:25, one launch (start us, length us, event | category | flops | bytes accessed | tf_op | source)
XLA Modules:
  0.0 285.1 jit_solution(17261700212546261711)
XLA Ops:
  7.2 1.0 convert_reduce_fusion
  11.4 12.9 %all-to-all-start.1 = ((f32[32,32,2]{1,2,0:T(2,128)}), f32[32,32,2]{1,2,0:T(2,128)S(1)}, u32[]{:S(2)}, u32[]{:S(2)}) async-start(f32[32,32,2]{1,2,0:T(2,128)} %copy.63), calls=%async_computation.2 | async-start | bytes 65536 | tf_op jit(solution)/shard_map/all_to_all | solution.py:43
  24.3 1.5 convolution_convert_fusion.1
  26.7 6.4 %all-to-all-done.1 = f32[32,32,2]{1,2,0:T(2,128)S(1)} async-done(((f32[32,32,2]{1,2,0:T(2,128)}), f32[32,32,2]{1,2,0:T(2,128)S(1)}, u32[]{:S(2)}, u32[]{:S(2)}) %all-to-all-start.1) | async-done | bytes 8224 | tf_op jit(solution)/shard_map/all_to_all | solution.py:43
  33.0 4.6 %all-to-all-start.2 = ((bf16[32,32,2,128]{3,1,2,0:T(8,128)(2,1)}), bf16[32,32,2,128]{3,1,2,0:T(8,128)(2,1)}, u32[]{:S(2)}, u32[]{:S(2)}) async-start(bf16[32,32,2,128]{3,1,2,0:T(8,128)(2,1)} %copy.68), calls=%async_computation.3 | async-start | bytes 1048576 | tf_op jit(solution)/shard_map/all_to_all | solution.py:43
  38.5 1.6 copy.61
  40.1 12.2 %all-to-all-done.2 = bf16[32,32,2,128]{3,1,2,0:T(8,128)(2,1)} async-done(((bf16[32,32,2,128]{3,1,2,0:T(8,128)(2,1)}), bf16[32,32,2,128]{3,1,2,0:T(8,128)(2,1)}, u32[]{:S(2)}, u32[]{:S(2)}) %all-to-all-start.2) | async-done | bytes 524320 | tf_op jit(solution)/shard_map/all_to_all | solution.py:43
  52.3 6.4 %all-to-all-start = ((bf16[32,32,2,512]{3,1,2,0:T(8,128)(2,1)}), bf16[32,32,2,512]{3,1,2,0:T(8,128)(2,1)}, u32[]{:S(2)}, u32[]{:S(2)}) async-start(bf16[32,32,2,512]{3,1,2,0:T(8,128)(2,1)} %copy.61), calls=%async_computation.1 | async-start | bytes 4194304 | tf_op jit(solution)/shard_map/all_to_all | solution.py:43
  59.2 1.4 gather_fusion.1
  60.6 2.0 gather_fusion
  63.1 1.7 fusion.44
  64.8 39.7 %all-to-all-done = bf16[32,32,2,512]{3,1,2,0:T(8,128)(2,1)} async-done(((bf16[32,32,2,512]{3,1,2,0:T(8,128)(2,1)}), bf16[32,32,2,512]{3,1,2,0:T(8,128)(2,1)}, u32[]{:S(2)}, u32[]{:S(2)}) %all-to-all-start) | async-done | bytes 2097184 | tf_op jit(solution)/shard_map/all_to_all | solution.py:43
  104.5 3.0 %fusion.12 = f32[32,32,2,64]{3,1,2,0:T(8,128)S(1)} fusion(bf16[32,32,2,512]{3,1,2,0:T(8,128)(2,1)} %all-to-all-done, bf16[32,512,64]{1,2,0:T(8,128)(2,1)} %gather_fusion, pred[32]{0:T(512)(128)(4,1)S(1)} %get-tuple-element.18), kind=kOutput, calls=%fused_computation.15 | convolution fusion | flops 135266304 | bytes 4718624 | tf_op jit(solution)/shard_map/gjsd,gdr->gjsr/dot_general | solution.py:64
  107.5 1.3 pad_maximum_fusion
  108.9 4.2 %fusion.14 = f32[256,2,2048]{2,0,1:T(8,128)} fusion(bf16[512,2048]{1,0:T(8,128)(2,1)S(1)} %copy-done, bf16[256,2,512]{2,1,0:T(2,128)(2,1)} %param.9), kind=kOutput, calls=%fused_computation.17 | convolution fusion | flops 1073741824 | bytes 6815744 | tf_op jit(solution)/shard_map/asd,dk->ask/dot_general | solution.py:48
  113.3 95.3 %all-gather.3.cloned.1.call-done = f32[512,32,2,128]{3,1,2,0:T(8,128)} async-done(((f32[32,32,2,128]{3,1,2,0:T(8,128)}), f32[512,32,2,128]{3,1,2,0:T(8,128)}) %all-gather.3.cloned.1.call-update) | async-done | bytes 16777232 | tf_op jit(solution)/shard_map/all_gather | solution.py:67
  208.6 7.9 %reduce_sum.62 = bf16[32,32,2,128]{3,1,2,0:T(8,128)(2,1)S(1)} reduce(f32[16,32,32,2,128]{4,2,3,1,0:T(8,128)} %bitcast.76, f32[]{:T(128)} %constant.65.clone.1), dimensions={0}, to_apply=%region_6.7 | reduce | flops 3932160 | bytes 17301508 | tf_op jit(solution)/shard_map/reduce_sum | solution.py:66
  216.6 1.2 fusion.27
  217.7 10.1 %all-to-all-start.3 = ((bf16[32,32,2,128]{3,1,2,0:T(8,128)(2,1)}), bf16[32,32,2,128]{3,1,2,0:T(8,128)(2,1)S(1)}, u32[]{:S(2)}, u32[]{:S(2)}) async-start(bf16[32,32,2,128]{3,1,2,0:T(8,128)(2,1)} %fusion.27), calls=%async_computation.4 | async-start | bytes 1048576 | tf_op jit(solution)/shard_map/all_to_all | solution.py:43
  228.1 7.1 %fusion.22 = bf16[16,512,64]{1,2,0:T(8,128)(2,1)} fusion(bf16[32,32,2,512]{3,1,2,0:T(8,128)(2,1)} %all-to-all-done, pred[32,16]{1,0:T(8,128)(4,1)S(1)} %iota_compare_fusion.6, bf16[32,32,2,64]{3,1,2,0:T(8,128)(2,1)S(1)} %get-tuple-element.21), kind=kOutput, calls=%fused_computation.24 | convolution fusion | flops 2150629376 | bytes 3408384 | tf_op jit(solution)/shard_map/gjsd,gjstr->tdr/dot_general | solution.py:76
  235.1 4.9 %fusion.34 = bf16[16,64,128]{2,1,0:T(8,128)(2,1)} fusion(pred[32,16]{1,0:T(8,128)(4,1)S(1)} %iota_compare_fusion.6, bf16[32,32,2,64]{3,1,2,0:T(8,128)(2,1)S(1)} %get-tuple-element.20, bf16[32,32,2,128]{3,1,2,0:T(8,128)(2,1)} %all-to-all-done.2, f32[32,32]{1,0:T(8,128)S(1)} %multiply_subtract_fusion), kind=kOutput, calls=%fused_computation.29 | convolution fusion | flops 540016640 | bytes 1053184 | tf_op jit(solution)/shard_map/gjstr,gjsk->trk/dot_general | solution.py:78
  240.0 4.2 %all-to-all-done.3 = bf16[32,32,2,128]{3,1,2,0:T(8,128)(2,1)S(1)} async-done(((bf16[32,32,2,128]{3,1,2,0:T(8,128)(2,1)}), bf16[32,32,2,128]{3,1,2,0:T(8,128)(2,1)S(1)}, u32[]{:S(2)}, u32[]{:S(2)}) %all-to-all-start.3) | async-done | bytes 524320 | tf_op jit(solution)/shard_map/all_to_all | solution.py:43
  244.3 31.9 %reduce-scatter.2.cloned.1.call-done = f32[256,2,128]{2,0,1:T(8,128)} async-done(((f32[256,2,2048]{2,0,1:T(8,128)}), f32[256,2,128]{2,0,1:T(8,128)}) %reduce-scatter.2.cloned.1.call-update) | async-done | bytes 262160 | tf_op jit(solution)/shard_map/reduce_scatter | solution.py:49
  276.2 1.3 fusion.37
  (44 shorter events, 7.0 us)
Async XLA Ops:
  7.2 101.8 %copy-start = (bf16[512,2048]{1,0:T(8,128)(2,1)S(1)}, bf16[512,2048]{1,0:T(8,128)(2,1)}, u32[]{:S(2)}) copy-start(bf16[512,2048]{1,0:T(8,128)(2,1)} %param.10) | copy-start | bytes 6291460
  7.2 30.5 %copy-start.3 = (bf16[256,2,512]{2,1,0:T(2,128)(2,1)S(1)}, bf16[256,2,512]{2,1,0:T(2,128)(2,1)}, u32[]{:S(2)}) copy-start(bf16[256,2,512]{2,1,0:T(2,128)(2,1)} %param.9) | copy-start | bytes 1572868
  11.4 21.6 %all-to-all-start.1 = ((f32[32,32,2]{1,2,0:T(2,128)}), f32[32,32,2]{1,2,0:T(2,128)S(1)}, u32[]{:S(2)}, u32[]{:S(2)}) async-start(f32[32,32,2]{1,2,0:T(2,128)} %copy.63), calls=%async_computation.2 | async-start | bytes 65536 | tf_op jit(solution)/shard_map/all_to_all | solution.py:43
  33.0 19.3 %all-to-all-start.2 = ((bf16[32,32,2,128]{3,1,2,0:T(8,128)(2,1)}), bf16[32,32,2,128]{3,1,2,0:T(8,128)(2,1)}, u32[]{:S(2)}, u32[]{:S(2)}) async-start(bf16[32,32,2,128]{3,1,2,0:T(8,128)(2,1)} %copy.68), calls=%async_computation.3 | async-start | bytes 1048576 | tf_op jit(solution)/shard_map/all_to_all | solution.py:43
  40.1 18.7 %copy-start.5 = (s32[32,32]{1,0:T(8,128)S(1)}, s32[32,32]{1,0:T(8,128)}, u32[]{:S(2)}) copy-start(s32[32,32]{1,0:T(8,128)} %param.14) | copy-start | bytes 12292
  40.1 18.9 %copy-start.6 = (s32[512]{0:T(512)S(1)}, s32[512]{0:T(512)}, u32[]{:S(2)}) copy-start(s32[512]{0:T(512)} %param.15) | copy-start | bytes 6148
  40.1 19.1 %copy-start.4 = (bf16[16,64,128]{2,1,0:T(8,128)(2,1)S(1)}, bf16[16,64,128]{2,1,0:T(8,128)(2,1)}, u32[]{:S(2)}) copy-start(bf16[16,64,128]{2,1,0:T(8,128)(2,1)} %param.12) | copy-start | bytes 786436
  40.1 20.5 %copy-start.1 = (bf16[16,512,64]{1,2,0:T(8,128)(2,1)S(1)}, bf16[16,512,64]{1,2,0:T(8,128)(2,1)}, u32[]{:S(2)}) copy-start(bf16[16,512,64]{1,2,0:T(8,128)(2,1)} %param.11) | copy-start | bytes 3145732
  52.3 52.3 %all-to-all-start = ((bf16[32,32,2,512]{3,1,2,0:T(8,128)(2,1)}), bf16[32,32,2,512]{3,1,2,0:T(8,128)(2,1)}, u32[]{:S(2)}, u32[]{:S(2)}) async-start(bf16[32,32,2,512]{3,1,2,0:T(8,128)(2,1)} %copy.61), calls=%async_computation.1 | async-start | bytes 4194304 | tf_op jit(solution)/shard_map/all_to_all | solution.py:43
  58.7 149.9 %all-gather.3.cloned.1.call-start = ((), (), s32[]{:S(2)}) async-start(), calls=%async_computation.6 | async-start | bytes 17825792 | tf_op jit(solution)/shard_map/all_gather | solution.py:67
  108.9 167.3 %reduce-scatter.2.cloned.1.call-start = ((), (), s32[]{:S(2)}) async-start(), calls=%async_computation.5 | async-start | bytes 4456448 | tf_op jit(solution)/shard_map/reduce_scatter | solution.py:49
  208.6 7.9 %copy-start.2 = (bf16[32,64,128]{2,1,0:T(8,128)(2,1)S(1)}, bf16[32,64,128]{2,1,0:T(8,128)(2,1)}, u32[]{:S(2)}) copy-start(bf16[32,64,128]{2,1,0:T(8,128)(2,1)} %gather_fusion.1) | copy-start | bytes 1572868
  217.7 26.5 %all-to-all-start.3 = ((bf16[32,32,2,128]{3,1,2,0:T(8,128)(2,1)}), bf16[32,32,2,128]{3,1,2,0:T(8,128)(2,1)S(1)}, u32[]{:S(2)}, u32[]{:S(2)}) async-start(bf16[32,32,2,128]{3,1,2,0:T(8,128)(2,1)} %fusion.27), calls=%async_computation.4 | async-start | bytes 1048576 | tf_op jit(solution)/shard_map/all_to_all | solution.py:43
Sparse Core Ops, SparseCore 0:
  109.0 99.5 all-gather.2
  211.5 64.6 reduce-scatter.1
